TPU v7x, 32 devices: a whole 2x2x4 slice. The times are simulated.
32 devices in a mesh: ctx: 16 (over z, x, core), cand: 2 (over y).
Axes of the slice: x: 2, y: 2, z: 4, core: 2. Of those that a mesh axis runs over, the one named last changes fastest.
Arguments:
- queries: bfloat16 [512, 1024], P(('cand', 'ctx')), may hold values from -256 to 256
- grad_out: bfloat16 [512, 1024], P(('cand', 'ctx')), may hold values from -6 to 6
- prefix_keys: bfloat16 [16384, 128], P(('ctx', 'cand')), may hold values from -4 to 4
- prefix_values: bfloat16 [16384, 128], P(('ctx', 'cand')), may hold values from -6 to 6
- cand_keys: bfloat16 [512, 128], P('cand'), may hold values from -6 to 6
- cand_values: bfloat16 [512, 128], P('cand'), may hold values from -6 to 6
- lengths: int32 [2, 4], P('cand'), may hold values from 1 to 128, 256 in all within a row
- offsets: int32 [8], P('cand'), may hold values from 4096 to 16384
Outputs:
- grad_queries: bfloat16 [512, 1024], P(('cand', 'ctx'))
- grad_keys: bfloat16 [16384, 128], P(('ctx', 'cand'))
- grad_values: bfloat16 [16384, 128], P(('ctx', 'cand'))
Inputs may be any that keep to these rules, and one draw needn't show every extreme that they name: Each row of lengths sums to 256.
All inputs are finite; a program needn't handle non-finite values.
Results may differ from a plain program's by a relative error of at most 0.015.
Values may be sent and summed in bfloat16 or wider, within the bound.
No kernel may reach another device: no remote copies, remote signals or barrier semaphores. Data moves between devices by JAX's collectives and lax.ppermute only.
A program may use at most 64 MiB of HBM per device.

v0:
```python
import math

import jax
import jax.numpy as jnp
from jax import lax
from jax.sharding import PartitionSpec as P

HEADS = 8
HD = 128


NEG = -1e30


def merged(array, axis, combine):
    everything = jax.tree.map(lambda part: lax.all_gather(part, axis), array)
    leading = jax.tree.map(lambda part: part[0], everything)

    def turn(k, so_far):
        return combine(so_far, jax.tree.map(lambda part: part[k], everything))

    return lax.fori_loop(1, lax.axis_size(axis), turn, leading)


def spread(weights, values):
    return weights.reshape(weights.shape + (1,) * (values.ndim - 1))


def combine(former, latter):
    highest = jnp.maximum(former[0], latter[0])
    former_weight = jnp.exp(former[0] - highest)
    latter_weight = jnp.exp(latter[0] - highest)
    totals = former[1] * former_weight + latter[1] * latter_weight
    carried = former[2] * spread(former_weight, former[2]) + latter[2] * spread(
        latter_weight, latter[2]
    )
    return (highest, totals, carried)


def body(queries, grad_out, prefix_keys, prefix_values, cand_keys, cand_values, lengths, offsets):
    scaling = 1.0 / math.sqrt(HD)
    owned = queries.shape[0]
    block_len = cand_keys.shape[0]
    ctx_index = lax.axis_index("ctx")
    keys_here, values_here = (
        lax.all_gather(prefix_keys, "cand", axis=0, tiled=True),
        lax.all_gather(prefix_values, "cand", axis=0, tiled=True),
    )
    key_count = keys_here.shape[0]
    query_block, grad_block = (
        lax.all_gather(queries, "ctx", axis=0, tiled=True),
        lax.all_gather(grad_out, "ctx", axis=0, tiled=True),
    )
    ends = jnp.cumsum(lengths[0])
    tokens_local = jnp.arange(block_len, dtype=jnp.int32)
    segment = jnp.sum((tokens_local[:, None] >= ends[None, :]).astype(jnp.int32), axis=1)
    matches = segment[:, None] == jnp.arange(ends.shape[0], dtype=jnp.int32)[None, :]
    limit = jnp.sum(jnp.where(matches, offsets[None, :], 0), axis=1)
    row_count = block_len * HEADS
    limit_rows = jnp.broadcast_to(limit[:, None], (block_len, HEADS)).reshape(row_count)
    first_key = ctx_index * key_count
    position = first_key + jnp.arange(key_count, dtype=jnp.int32)
    query_rows = query_block.reshape(row_count, HD)
    grad_rows = grad_block.reshape(row_count, HD)
    block_rows = math.gcd(row_count, 512)
    block_total = row_count // block_rows

    def forward_rows(bundle):
        rows_query, rows_grad, rows_limit = bundle
        scores = jnp.dot(rows_query, keys_here.T, preferred_element_type=jnp.float32) * scaling
        visible = position[None, :] < rows_limit[:, None]
        highest = jnp.max(jnp.where(visible, scores, NEG), axis=1)
        expon = jnp.where(visible, jnp.exp(scores - highest[:, None]), 0.0)
        totals = jnp.sum(expon, axis=1)
        products = jnp.dot(rows_grad, values_here.T, preferred_element_type=jnp.float32)
        carried = jnp.sum(expon * products, axis=1)
        return (highest, totals, carried)

    def forward_block(bundle):
        return forward_rows(bundle)

    blocked = (
        query_rows.reshape(block_total, block_rows, HD),
        grad_rows.reshape(block_total, block_rows, HD),
        limit_rows.reshape(block_total, block_rows),
    )
    stat_high, stat_total, stat_carry = lax.map(forward_block, blocked)
    stat_high = stat_high.reshape(row_count)
    stat_total = stat_total.reshape(row_count)
    stat_carry = stat_carry.reshape((row_count,) + stat_carry.shape[2:])
    own_rows = owned * HEADS
    row_start = ctx_index * own_rows
    token_start = ctx_index * owned
    own_query = queries.reshape(own_rows, HD)
    own_grad = grad_out.reshape(own_rows, HD)
    own_tokens = token_start + jnp.arange(owned, dtype=jnp.int32)
    own_segment = lax.dynamic_slice_in_dim(segment, token_start, owned)
    allowed = (own_segment[:, None] == segment[None, :]) & (
        tokens_local[None, :] <= own_tokens[:, None]
    )
    allowed_rows = jnp.broadcast_to(allowed[:, None, :], (owned, HEADS, block_len)).reshape(
        own_rows, block_len
    )
    self_scores = jnp.dot(own_query, cand_keys.T, preferred_element_type=jnp.float32) * scaling
    self_high = jnp.max(jnp.where(allowed_rows, self_scores, NEG), axis=1)
    self_exp = jnp.where(allowed_rows, jnp.exp(self_scores - self_high[:, None]), 0.0)
    self_products = jnp.dot(own_grad, cand_values.T, preferred_element_type=jnp.float32)
    self_carry = jnp.sum(self_exp * self_products, axis=1)
    prefix_own = tuple(
        (
            lax.dynamic_slice_in_dim(whole, row_start, own_rows, 0)
            for whole in (stat_high, stat_total, stat_carry)
        )
    )
    joined = combine(prefix_own, (self_high, jnp.sum(self_exp, axis=1), self_carry))
    stats = tuple(
        (
            lax.dynamic_update_slice_in_dim(whole, piece, row_start, 0)
            for whole, piece in zip((stat_high, stat_total, stat_carry), joined)
        )
    )
    highest, totals, carried = merged(stats, "ctx", combine)
    delta = carried / totals

    def backward_rows(bundle):
        rows_query, rows_grad, rows_limit, rows_high, rows_total, rows_delta = bundle
        scores = jnp.dot(rows_query, keys_here.T, preferred_element_type=jnp.float32) * scaling
        visible = position[None, :] < rows_limit[:, None]
        probs = jnp.where(visible, jnp.exp(scores - rows_high[:, None]), 0.0) / rows_total[:, None]
        products = jnp.dot(rows_grad, values_here.T, preferred_element_type=jnp.float32)
        slopes = (probs * (products - rows_delta[:, None])).astype(jnp.bfloat16)
        return (probs.astype(jnp.bfloat16), slopes)

    def backward_block(bundle):
        return backward_rows(bundle)

    probs_low, slopes = lax.map(
        backward_block,
        blocked
        + (
            highest.reshape(block_total, block_rows),
            totals.reshape(block_total, block_rows),
            delta.reshape(block_total, block_rows),
        ),
    )
    probs_low = probs_low.reshape(row_count, key_count)
    slopes = slopes.reshape(row_count, key_count)
    prefix_grad = lax.psum_scatter(
        (scaling * jnp.dot(slopes, keys_here, preferred_element_type=jnp.float32))
        .reshape(lax.axis_size("ctx") * owned, HEADS * HD)
        .astype(jnp.bfloat16),
        "ctx",
        scatter_dimension=0,
        tiled=True,
    ).astype(jnp.float32)
    own_high = lax.dynamic_slice_in_dim(highest, row_start, own_rows, 0)
    own_total = lax.dynamic_slice_in_dim(totals, row_start, own_rows, 0)
    own_delta = lax.dynamic_slice_in_dim(delta, row_start, own_rows, 0)
    self_probs = (
        jnp.where(allowed_rows, jnp.exp(self_scores - own_high[:, None]), 0.0) / own_total[:, None]
    )
    self_slopes = (self_probs * (self_products - own_delta[:, None])).astype(jnp.bfloat16)
    self_grad = (
        scaling * jnp.dot(self_slopes, cand_keys, preferred_element_type=jnp.float32)
    ).reshape(owned, HEADS * HD)
    grad_queries = (prefix_grad + self_grad).astype(jnp.bfloat16)
    contract = (((0,), (0,)), ((), ()))
    key_part = scaling * lax.dot_general(
        slopes, query_rows, contract, preferred_element_type=jnp.float32
    )
    value_part = lax.dot_general(probs_low, grad_rows, contract, preferred_element_type=jnp.float32)
    key_value_grads = lax.psum_scatter(
        jnp.concatenate([key_part, value_part], axis=1).astype(jnp.bfloat16),
        "cand",
        scatter_dimension=0,
        tiled=True,
    ).astype(jnp.float32)
    grad_keys = key_value_grads[:, :HD].astype(jnp.bfloat16)
    grad_values = key_value_grads[:, HD:].astype(jnp.bfloat16)
    return (grad_queries, grad_keys, grad_values)


def solution(mesh):
    placed = (
        P(("cand", "ctx"), None),
        P(("cand", "ctx"), None),
        P(("ctx", "cand"), None),
        P(("ctx", "cand"), None),
        P("cand", None),
        P("cand", None),
        P("cand", None),
        P("cand"),
    )
    return jax.shard_map(
        body,
        mesh=mesh,
        in_specs=placed,
        out_specs=(P(("cand", "ctx"), None), P(("ctx", "cand"), None), P(("ctx", "cand"), None)),
        check_vma=False,
    )
```

profile of v0, /device:TPU:0, one launch (start us, length us, event | category | flops | bytes accessed | tf_op | source)
XLA Modules:
  0.0 231.7 jit_solution(4950674165554086775)
XLA Ops:
  8.1 24.8 %all_gather.36 = bf16[256,1024]{1,0:T(8,128)(2,1)S(1)} all-gather(bf16[16,1024]{1,0:T(8,128)(2,1)} %param.14), channel_id=1, replica_groups=mesh['ctx'=16,'cand'=2] {'ctx'}, dimensions={0}, use_global_device_ids=true | all-gather | bytes 557056 | tf_op jit(solution)/shard_map/all_gather | solution.py:51
  33.7 19.1 %all_gather.38 = bf16[256,1024]{1,0:T(8,128)(2,1)S(1)} all-gather(bf16[16,1024]{1,0:T(8,128)(2,1)} %param.15), channel_id=1, replica_groups=mesh['ctx'=16,'cand'=2] {'ctx'}, dimensions={0}, use_global_device_ids=true | all-gather | bytes 557056 | tf_op jit(solution)/shard_map/all_gather | solution.py:52
  54.8 6.6 %all_gather.37 = bf16[1024,128]{1,0:T(8,128)(2,1)S(1)} all-gather(bf16[512,128]{1,0:T(8,128)(2,1)} %param.16), channel_id=1, replica_groups=mesh['ctx'=16,'cand'=2] {'cand'}, dimensions={0}, use_global_device_ids=true | all-gather | bytes 393216 | tf_op jit(solution)/shard_map/all_gather | solution.py:46
  61.4 5.8 %all_gather.39 = bf16[1024,128]{1,0:T(8,128)(2,1)S(1)} all-gather(bf16[512,128]{1,0:T(8,128)(2,1)} %param.17), channel_id=1, replica_groups=mesh['ctx'=16,'cand'=2] {'cand'}, dimensions={0}, use_global_device_ids=true | all-gather | bytes 393216 | tf_op jit(solution)/shard_map/all_gather | solution.py:47
  67.7 8.9 %while.48 = (s32[]{:T(128)}, f32[4,512]{1,0:T(4,128)S(1)}, f32[4,512]{1,0:T(4,128)S(1)}, f32[4,512]{1,0:T(4,128)S(1)}, s32[4,512]{1,0:T(4,128)S(1)}, /*index=5*/...) while((s32[]{:T(128)}, f32[4,512]{1,0:T(4,128)S(1)}, ...), condition=%wide.region_7.8_spmd.clone, body=%wide.region_3.7_spmd.clone.sunk | while | flops 276299264 | bytes 7127193 | solution.py:87
  77.5 19.1 %all-gather.2 = f32[16,1,2048]{2,1,0:T(1,128)S(1)} all-gather(f32[1,1,2048]{2,1,0:T(1,128)S(1)} %get-tuple-element.440), channel_id=1, replica_groups=mesh['ctx'=16,'cand'=2] {'ctx'}, dimensions={0}, use_global_device_ids=true | all-gather | bytes 139264 | tf_op jit(solution)/shard_map/all_gather | solution.py:16
  96.6 17.8 %all-gather.1 = f32[16,1,2048]{2,1,0:T(1,128)S(1)} all-gather(f32[1,1,2048]{2,1,0:T(1,128)S(1)} %get-tuple-element.441), channel_id=1, replica_groups=mesh['ctx'=16,'cand'=2] {'ctx'}, dimensions={0}, use_global_device_ids=true | all-gather | bytes 139264 | tf_op jit(solution)/shard_map/all_gather | solution.py:16
  114.5 19.1 %all-gather = f32[16,1,2048]{2,1,0:T(1,128)S(1)} all-gather(f32[1,1,2048]{2,1,0:T(1,128)S(1)} %get-tuple-element.442), channel_id=1, replica_groups=mesh['ctx'=16,'cand'=2] {'ctx'}, dimensions={0}, use_global_device_ids=true | all-gather | bytes 139264 | tf_op jit(solution)/shard_map/all_gather | solution.py:16
  133.6 1.8 while.47
  135.5 12.8 %while.49 = (s32[]{:T(128)}, bf16[4,512,1024]{2,1,0:T(8,128)(2,1)}, bf16[4,512,1024]{2,1,0:T(8,128)(2,1)}, s32[4,512]{1,0:T(4,128)S(1)}, bf16[4,512,128]{2,1,0:T...) while((s32[]{:T(128)}, bf16[4,512,1024]{2,1,0:T(8,128)(2,1)}, ...), condition=%wide.region_14.15_spmd.clone, body=%wide.region_13.14_spmd.clone.sunk | while | flops 273155072 | bytes 7112853 | solution.py:137
  135.6 1.7 bitcast_dynamic-update-slice_fusion.2
  137.3 1.4 fusion.64
  138.8 1.7 bitcast_dynamic-update-slice_fusion.2
  140.5 1.5 fusion.64
  142.0 1.7 bitcast_dynamic-update-slice_fusion.2
  143.7 1.4 fusion.64
  145.2 1.7 bitcast_dynamic-update-slice_fusion.2
  146.9 1.4 fusion.64
  148.3 3.4 %fusion.21 = bf16[2048,128]{1,0:T(8,128)(2,1)S(1)} fusion(bf16[2048,1024]{1,0:T(8,128)(2,1)} %bitcast.161, bf16[1024,128]{1,0:T(8,128)(2,1)S(1)} %get-tuple-element.758), kind=kOutput, calls=%fused_computation.40 | convolution fusion | flops 537395200 | bytes 4980736 | tf_op jit(solution)/shard_map/dot_general | solution.py:149
  151.7 1.1 convert_element_type.30
  153.4 3.1 %convolution_convert_fusion = bf16[1024,128]{0,1:T(8,128)(2,1)S(1)} fusion(bf16[2048,1024]{1,0:T(8,128)(2,1)} %bitcast.164, bf16[2048,128]{1,0:T(8,128)(2,1)S(1)} %reshape.166), kind=kOutput, calls=%fused_computation.43 | convolution fusion | flops 537001984 | bytes 4980736 | tf_op jit(solution)/shard_map/dot_general | solution.py:171
  159.0 47.5 %reduce-scatter.3.cloned.1.call-done = bf16[16,1024]{1,0:T(8,128)(2,1)} async-done(((bf16[256,1024]{1,0:T(8,128)(2,1)}), bf16[16,1024]{1,0:T(8,128)(2,1)}) %reduce-scatter.3.cloned.1.call-update) | async-done | bytes 32784 | tf_op jit(solution)/shard_map/reduce_scatter | solution.py:148
  206.5 1.4 add_convert_fusion
  207.8 14.6 %reduce-scatter.5.cloned.1.call-done = bf16[512,256]{0,1:T(8,128)(2,1)} async-done(((bf16[1024,256]{0,1:T(8,128)(2,1)}), bf16[512,256]{0,1:T(8,128)(2,1)}) %reduce-scatter.5.cloned.1.call-update) | async-done | bytes 262160 | tf_op jit(solution)/shard_map/reduce_scatter | solution.py:172
  (182 shorter events, 20.4 us)
Async XLA Ops:
  7.2 69.7 %copy-start = (bf16[256,128]{1,0:T(8,128)(2,1)S(1)}, bf16[256,128]{1,0:T(8,128)(2,1)}, u32[]{:S(2)}) copy-start(bf16[256,128]{1,0:T(8,128)(2,1)} %param.18) | copy-start | bytes 196612
  7.2 199.3 %reduce-scatter.3.cloned.1.call-start = ((), (), s32[]{:S(2)}) async-start(), calls=%async_computation.2 | async-start | bytes 557056 | tf_op jit(solution)/shard_map/reduce_scatter | solution.py:148
  67.7 9.4 %copy-start.1 = (bf16[256,128]{1,0:T(8,128)(2,1)S(1)}, bf16[256,128]{1,0:T(8,128)(2,1)}, u32[]{:S(2)}) copy-start(bf16[256,128]{1,0:T(8,128)(2,1)} %param.19) | copy-start | bytes 196612
  152.8 69.6 %reduce-scatter.5.cloned.1.call-start = ((), (), s32[]{:S(2)}) async-start(), calls=%async_computation.3 | async-start | bytes 786432 | tf_op jit(solution)/shard_map/reduce_scatter | solution.py:172
  153.4 3.5 %copy-start.2 = (bf16[4,512,1024]{2,1,0:T(8,128)(2,1)S(1)}, bf16[4,512,1024]{2,1,0:T(8,128)(2,1)}, u32[]{:S(2)}) copy-start(bf16[4,512,1024]{2,1,0:T(8,128)(2,1)} %get-tuple-element.304) | copy-start | bytes 12582916
Sparse Core Ops, SparseCore 0:
  153.0 53.4 reduce-scatter.2
  208.7 13.6 reduce-scatter.4
where the time goes:
time: 232 us
  blocking collectives  112 us (48%)
  waiting for transfers between devices  62.1 us (27%)
  matrix products  26.1 us (11%)
  between operations  14.3 us (6%)
  local copies, waits for them, and re-layouts  8.56 us (4%)
  other arithmetic  7.22 us (3%)
    all_gather x3, blocking collectives, merged(): everything = jax.tree.map(lambda part: lax.all_gather(part, axis), array)  56 us
    reduce_scatter x1, waiting for transfers between devices, body(): lax.psum_scatter((scaling * jnp.dot(slopes, keys_here, preferred_element_...  47.5 us
    all_gather x1, blocking collectives, body(): lax.all_gather(queries, 'ctx', axis=0, tiled=True)  24.8 us
    all_gather x1, blocking collectives, body(): lax.all_gather(grad_out, 'ctx', axis=0, tiled=True)  19.1 us
    reduce_scatter x1, waiting for transfers between devices, body(): lax.psum_scatter(jnp.concatenate([key_part, value_part], axis=1).astype(j...  14.6 us
    dot_general x4, matrix products, backward_rows(): jnp.dot(rows_query, keys_here.T, preferred_element_type=jnp.float32)  6.83 us
    all_gather x1, blocking collectives, body(): lax.all_gather(prefix_keys, 'cand', axis=0, tiled=True)  6.63 us
    all_gather x1, blocking collectives, body(): lax.all_gather(prefix_values, 'cand', axis=0, tiled=True)  5.84 us
  transfers between devices with their start and end apart: 2, of which 2 were waited for; matrix products, arithmetic and copies ran while one was open for 3% of the time, Pallas kernels for 0%

commit v1 on v0

v1 whole, which is shorter than its diff:
```python
import functools
import itertools
import math

import jax
import jax.numpy as jnp
from jax import lax
from jax.experimental import pallas as pl
from jax.experimental.pallas import tpu as pltpu
from jax.sharding import PartitionSpec as P

HEADS = 8
HD = 128
NEG = -1e30
SCALING = 1.0 / math.sqrt(HD)
RATE = SCALING * math.log2(math.e)
BOTH = ("ctx", "cand")
NT = (((1,), (1,)), ((), ()))
TN = (((0,), (0,)), ((), ()))


class Layout:
    def __init__(self, mesh):
        ctx, self.cand = mesh.shape["ctx"], mesh.shape["cand"]
        self.core = 2
        self.x = 2
        self.z = ctx // (self.core * self.x)

    def linear(self, z, x, core, cand):
        return ((z * self.x + x) * self.core + core) * self.cand + cand

    def permute(self, array, dz=0, dx=0, dcore=0, dcand=0):
        places = itertools.product(*map(range, (self.z, self.x, self.core, self.cand)))
        pairs = [
            (self.linear(z, x, c, y), self.linear(z ^ dz, x ^ dx, c ^ dcore, y ^ dcand))
            for z, x, c, y in places
        ]
        return lax.ppermute(array, BOTH, pairs)

    def key_steps(self):
        return [(dx, dy) for dx in range(self.x) for dy in range(self.cand)]

    def here(self):
        ctx, cand = lax.axis_index("ctx"), lax.axis_index("cand")
        core = ctx % self.core
        x = (ctx // self.core) % self.x
        z = ctx // (self.core * self.x)
        return z, x, core, cand


def token_limits(layout, owned, here, lengths_ref, offsets_ref):
    z, x, core, _ = here
    tokens = layout.z * layout.core * owned
    lane = lax.broadcasted_iota(jnp.int32, (1, tokens), 1)
    half = lane // (layout.z * owned)
    slot = (lane // owned) % layout.z
    place = ((jnp.bitwise_xor(slot, z) * layout.x + x) * layout.core) + jnp.bitwise_xor(half, core)
    pos = place * owned + lane % owned
    limit = jnp.full((1, tokens), offsets_ref[0], jnp.int32)
    start = jnp.zeros((1, tokens), jnp.int32)
    end = jnp.int32(0)
    for b in range(1, lengths_ref.shape[1]):
        end = end + lengths_ref[0, b - 1]
        later = pos >= end
        limit = jnp.where(later, offsets_ref[b], limit)
        start = jnp.where(later, end, start)
    return limit, start, pos


def pair(vector):
    return jnp.concatenate([vector, vector], axis=1)


def swap_lanes(vector, amount):
    lanes = vector.shape[-1]
    lane = lax.broadcasted_iota(jnp.int32, vector.shape, vector.ndim - 1)
    axis = vector.ndim - 1
    down = pltpu.roll(vector, lanes - amount, axis)
    if 2 * amount == lanes:
        return down
    return jnp.where((lane // amount) % 2 == 0, down, pltpu.roll(vector, amount, axis))


def rows_of(half_a, half_b, q_rows, g_rows):
    tokens = half_a.shape[0]
    for h in range(HEADS):
        lanes = slice(h * HD, (h + 1) * HD)
        upper = slice((HEADS + h) * HD, (HEADS + h + 1) * HD)
        for k, half in enumerate((half_a, half_b)):
            rows = slice(h * 2 * tokens + k * tokens, h * 2 * tokens + (k + 1) * tokens)
            q_rows[rows, :] = half[:, lanes]
            g_rows[rows, :] = half[:, upper]


def key_blocks(layout, here, key_refs, cand_keys, cand_values, limits):
    z, x, core, cand = here
    limit, start, pos = limits
    wide = 2 * limit.shape[1]
    limit2, start2, pos2 = pair(limit), pair(start), pair(pos)
    for (dx, dy), ref in zip(layout.key_steps(), key_refs):
        count = ref.shape[1]
        base = layout.linear(z, jnp.bitwise_xor(x, dx), core, jnp.bitwise_xor(cand, dy)) * count

        def visible(count=count, base=base):
            index = lax.broadcasted_iota(jnp.int32, (count, wide), 0)
            return index < (limit2 - base)

        yield ref[0], ref[1], visible
    count = cand_keys.shape[0] // (layout.z * layout.core)
    first = pl.multiple_of((z * layout.core + core) * count, count)

    def allowed():
        index = lax.broadcasted_iota(jnp.int32, (count, wide), 0) + first
        return (index >= start2) & (index <= pos2)

    yield cand_keys[pl.ds(first, count), :], cand_values[pl.ds(first, count), :], allowed


def forward_kernel(layout, owned, steps, *refs):
    lengths_ref, offsets_ref, half_a, half_b = refs[:4]
    key_refs, (cand_keys, cand_values) = refs[4 : 4 + steps], refs[4 + steps : 6 + steps]
    stats, stats_turned, q_rows, g_rows = refs[6 + steps :]
    here = layout.here()
    rows_of(half_a, half_b, q_rows, g_rows)
    limits = token_limits(layout, owned, here, lengths_ref, offsets_ref)
    tokens = limits[0].shape[1]
    total = [None] * (HEADS // 2)
    for keys, values, visible in key_blocks(layout, here, key_refs, cand_keys, cand_values, limits):
        seen = visible()
        for p in range(HEADS // 2):
            rows = slice(p * 2 * tokens, (p + 1) * 2 * tokens)
            scores = lax.dot_general(keys, q_rows[rows, :], NT, preferred_element_type=jnp.float32)
            products = lax.dot_general(values, g_rows[rows, :], NT, preferred_element_type=jnp.float32)
            scores = jnp.where(seen, scores, NEG)
            high = jnp.max(scores, axis=0, keepdims=True)
            if total[p] is not None:
                high = jnp.maximum(high, total[p][0])
            expon = jnp.exp2((scores - high) * RATE)
            mass = jnp.sum(expon, axis=0, keepdims=True)
            carry = jnp.sum(expon * products, axis=0, keepdims=True)
            if total[p] is not None:
                fade = jnp.exp2((total[p][0] - high) * RATE)
                mass = mass + fade * total[p][1]
                carry = carry + fade * total[p][2]
            total[p] = (high, mass, carry)
    for p in range(HEADS // 2):
        high, mass, carry = total[p]
        none = high <= NEG
        mass = jnp.where(none, 0.0, mass)
        carry = jnp.where(none, 0.0, carry)
        for k, value in enumerate((high, mass, carry)):
            stats[k, 2 * p : 2 * p + 1, :] = value[:, :tokens]
            stats[k, 2 * p + 1 : 2 * p + 2, :] = value[:, tokens:]
    for k in range(3):
        stats_turned[k] = swap_lanes(stats[k], tokens // 2)


def joined(parts):
    high = functools.reduce(jnp.maximum, [p[0] for p in parts])
    fades = [jnp.exp2((p[0] - high) * RATE) for p in parts]
    mass = sum(p[1] * f for p, f in zip(parts, fades))
    carry = sum(p[2] * f for p, f in zip(parts, fades))
    return high, mass, carry


def backward_kernel(layout, owned, steps, *refs):
    lengths_ref, offsets_ref, q_rows, g_rows = refs[:4]
    stat_refs = refs[4 : 4 + layout.z]
    at = 4 + layout.z
    key_refs, (cand_keys, cand_values) = refs[at : at + steps], refs[at + steps : at + steps + 2]
    at = at + steps + 2
    outs, (dq_own, dq_other) = refs[at : at + steps], refs[at + steps : at + steps + 2]
    probs, slopes, all_keys = refs[at + steps + 2 :]
    here = layout.here()
    limits = token_limits(layout, owned, here, lengths_ref, offsets_ref)
    tokens = limits[0].shape[1]
    parts = []
    for d, ref in enumerate(stat_refs):
        part = [ref[k] for k in range(3)]
        for bit in range(layout.z.bit_length()):
            if d >> bit & 1:
                part = [swap_lanes(value, owned << bit) for value in part]
        parts.append(part)
    high, mass, carry = joined(parts)
    shift = high + jnp.log2(mass) * (1.0 / RATE)
    delta = carry / mass

    def lanes_of(vector, p):
        return jnp.concatenate([vector[2 * p : 2 * p + 1], vector[2 * p + 1 : 2 * p + 2]], axis=1)

    done = 0
    blocks = key_blocks(layout, here, key_refs, cand_keys, cand_values, limits)
    for i, (keys, values, visible) in enumerate(blocks):
        count = keys.shape[0]
        seen = visible()
        all_keys[done : done + count, :] = keys
        for p in range(HEADS // 2):
            rows = slice(p * 2 * tokens, (p + 1) * 2 * tokens)
            scores = lax.dot_general(keys, q_rows[rows, :], NT, preferred_element_type=jnp.float32)
            products = lax.dot_general(values, g_rows[rows, :], NT, preferred_element_type=jnp.float32)
            scores = jnp.where(seen, scores, NEG)
            prob = jnp.exp2((scores - lanes_of(shift, p)) * RATE)
            slope = prob * (products - lanes_of(delta, p))
            slopes[done : done + count, rows] = slope.astype(jnp.bfloat16)
            if i < steps:
                probs[:, rows] = prob.astype(jnp.bfloat16)
        if i < steps:
            key_part = jnp.dot(
                slopes[done : done + count, :], q_rows[...], preferred_element_type=jnp.float32
            )
            value_part = jnp.dot(probs[...], g_rows[...], preferred_element_type=jnp.float32)
            outs[i][0] = (SCALING * key_part).astype(outs[i].dtype)
            outs[i][1] = value_part.astype(outs[i].dtype)
        done += count
    turned = lax.dot_general(all_keys[...], slopes[...], TN, preferred_element_type=jnp.float32)
    half = tokens // 2
    for h in range(HEADS):
        block = SCALING * jnp.transpose(turned[:, h * tokens : (h + 1) * tokens])
        dq_own[:, h * HD : (h + 1) * HD] = block[:half]
        dq_other[:, h * HD : (h + 1) * HD] = block[half:].astype(jnp.bfloat16)


def body(layout, queries, grad_out, prefix_keys, prefix_values, cand_keys, cand_values, lengths, offsets):
    owned = queries.shape[0]
    count = prefix_keys.shape[0]
    steps = layout.key_steps()
    pairs = jnp.stack([prefix_keys, prefix_values])
    key_sets = [pairs] + [layout.permute(pairs, dx=dx, dcand=dy) for dx, dy in steps[1:]]
    mine = jnp.concatenate([queries, grad_out], axis=1)
    half_a = jnp.concatenate([mine] + [layout.permute(mine, dz=d) for d in range(1, layout.z)], axis=0)
    half_b = layout.permute(half_a, dcore=1)
    tokens = 2 * half_a.shape[0]
    rows = tokens * HEADS
    vmem = pl.BlockSpec(memory_space=pltpu.VMEM)
    smem = pl.BlockSpec(memory_space=pltpu.SMEM)
    params = pltpu.CompilerParams(vmem_limit_bytes=40 * 1024 * 1024)
    stats, turned, q_rows, g_rows = pl.pallas_call(
        functools.partial(forward_kernel, layout, owned, len(steps)),
        out_shape=(
            jax.ShapeDtypeStruct((3, HEADS, tokens), jnp.float32),
            jax.ShapeDtypeStruct((3, HEADS, tokens), jnp.float32),
            jax.ShapeDtypeStruct((rows, HD), jnp.bfloat16),
            jax.ShapeDtypeStruct((rows, HD), jnp.bfloat16),
        ),
        in_specs=[smem, smem] + [vmem] * (4 + len(steps)),
        out_specs=(vmem,) * 4,
        compiler_params=params,
        name="forward",
    )(lengths, offsets, half_a, half_b, *key_sets, cand_keys, cand_values)
    stats = jnp.stack(joined([stats, layout.permute(turned, dcore=1)]))
    all_stats = [stats] + [layout.permute(stats, dz=d) for d in range(1, layout.z)]
    total_keys = count * len(steps) + cand_keys.shape[0] // (layout.z * layout.core)
    outs = pl.pallas_call(
        functools.partial(backward_kernel, layout, owned, len(steps)),
        out_shape=(
            [jax.ShapeDtypeStruct((2, count, HD), jnp.float32)]
            + [jax.ShapeDtypeStruct((2, count, HD), jnp.bfloat16)] * (len(steps) - 1)
            + [
                jax.ShapeDtypeStruct((tokens // 2, HEADS * HD), jnp.float32),
                jax.ShapeDtypeStruct((tokens // 2, HEADS * HD), jnp.bfloat16),
            ]
        ),
        in_specs=[smem, smem] + [vmem] * (4 + layout.z + len(steps)),
        out_specs=[vmem] * (len(steps) + 2),
        scratch_shapes=[
            pltpu.VMEM((count, rows), jnp.bfloat16),
            pltpu.VMEM((total_keys, rows), jnp.bfloat16),
            pltpu.VMEM((total_keys, HD), jnp.bfloat16),
        ],
        compiler_params=params,
        name="backward",
    )(lengths, offsets, q_rows, g_rows, *all_stats, *key_sets, cand_keys, cand_values)
    key_parts, (dq_own, dq_other) = outs[: len(steps)], outs[len(steps) :]
    key_value_grads = key_parts[0]
    for (dx, dy), part in zip(steps[1:], key_parts[1:]):
        key_value_grads = key_value_grads + layout.permute(part, dx=dx, dcand=dy).astype(jnp.float32)
    dq = dq_own + layout.permute(dq_other, dcore=1).astype(jnp.float32)
    grad_queries = dq[:owned]
    for d in range(1, layout.z):
        piece = dq[d * owned : (d + 1) * owned].astype(jnp.bfloat16)
        grad_queries = grad_queries + layout.permute(piece, dz=d).astype(jnp.float32)
    return (
        grad_queries.astype(jnp.bfloat16),
        key_value_grads[0].astype(jnp.bfloat16),
        key_value_grads[1].astype(jnp.bfloat16),
    )


def solution(mesh):
    placed = (
        P(("cand", "ctx"), None),
        P(("cand", "ctx"), None),
        P(("ctx", "cand"), None),
        P(("ctx", "cand"), None),
        P("cand", None),
        P("cand", None),
        P("cand", None),
        P("cand"),
    )
    return jax.shard_map(
        functools.partial(body, Layout(mesh)),
        mesh=mesh,
        in_specs=placed,
        out_specs=(P(("cand", "ctx"), None), P(("ctx", "cand"), None), P(("ctx", "cand"), None)),
        check_vma=False,
    )
```

time: 232 us -> 60.9 us (0.26)
  blocking collectives: 112 us -> 0 us
  waiting for transfers between devices: 62.1 us -> 24.4 us
  matrix products: 26.1 us -> 0 us
  starting transfers between devices: 0.08 us -> 20.8 us
  between operations: 14.3 us -> 0.79 us
  Pallas kernels: 0 us -> 10.6 us
  local copies, waits for them, and re-layouts: 8.56 us -> 2.31 us
  other arithmetic: 7.22 us -> 1.77 us
    all_gather x7 -> x0, blocking collectives: 112 us -> none  [the longest x3 56 us: merged(): everything = jax.tree.map(lambda part: lax.all_gather(part, axis), array)]
    reduce_scatter x2 -> x0, waiting for transfers between devices: 62 us -> none  [the longest x1 47.5 us: body(): lax.psum_scatter((scaling * jnp.dot(slopes, keys_here, preferred_element_...]
    dot_general x22 -> x0, matrix products: 26.1 us -> none  [the longest x4 6.83 us: backward_rows(): jnp.dot(rows_query, keys_here.T, preferred_element_type=jnp.float32)]
    ppermute x0 -> x18, waiting for transfers between devices: none -> 24.4 us  [permute(): return lax.ppermute(array, BOTH, pairs)]
    ppermute x0 -> x18, starting transfers between devices: none -> 20.8 us  [permute(): return lax.ppermute(array, BOTH, pairs)]
    pallas_call x0 -> x2, Pallas kernels: none -> 10.6 us  [the longest x1 6.06 us: body(): pl.pallas_call(functools.partial(backward_kernel, layout, owned, len(step...]
    reduce_sum x6 -> x0, other arithmetic: 3.55 us -> none  [the longest x4 2.72 us: forward_rows(): totals = jnp.sum(expon, axis=1)]
  transfers between devices with their start and end apart: 2 -> 18, of which waited for: 2 -> 10; matrix products, arithmetic and copies ran while one was open for 3% -> 3% of each run, Pallas kernels for 0% -> 0%
where the time goes in v1:
time: 60.9 us; the launch traced here: 60.6 us
  waiting for transfers between devices  24.4 us (40%)
  starting transfers between devices  20.8 us (34%)
  Pallas kernels  10.6 us (17%)
  local copies, waits for them, and re-layouts  2.31 us (4%)
  other arithmetic  1.77 us (3%)
  between operations  0.79 us (1%)
    ppermute x18, waiting for transfers between devices, permute(): return lax.ppermute(array, BOTH, pairs)  24.4 us
    ppermute x18, starting transfers between devices, permute(): return lax.ppermute(array, BOTH, pairs)  20.8 us
    pallas_call x1, Pallas kernels, body(): pl.pallas_call(functools.partial(backward_kernel, layout, owned, len(step...  6.06 us
    pallas_call x1, Pallas kernels, body(): pl.pallas_call(functools.partial(forward_kernel, layout, owned, len(steps...  4.49 us
  transfers between devices with their start and end apart: 18, of which 10 were waited for; matrix products, arithmetic and copies ran while one was open for 3% of the time, Pallas kernels for 0%

profile of v1, /device:TPU:0, one launch (start us, length us, event | category | flops | bytes accessed | tf_op | source)
XLA Modules:
  0.0 60.6 jit_solution(14734567057552194502)
XLA Ops:
  0.6 0.8 %constant_dynamic-update-slice_fusion.1 = bf16[16,2048]{1,0:T(8,128)(2,1)S(1)} fusion(bf16[16,1024]{1,0:T(8,128)(2,1)} %param.8), kind=kLoop, calls=%fused_computation.12 | loop fusion | bytes 65536
  1.4 0.8 %constant_dynamic-update-slice_fusion = bf16[16,2048]{1,0:T(8,128)(2,1)S(1)} fusion(bf16[16,2048]{1,0:T(8,128)(2,1)S(1)} %constant_dynamic-update-slice_fusion.1, bf16[16,1024]{1,0:T(8,128)(2,1)} %param.9), kind=kLoop, calls=%fused_computation.11 | loop fusion | bytes 65536 | tf_op jit(solution)/shard_map/concatenate | solution.py:229
  2.2 5.1 %collective-permute-start.2 = (bf16[16,2048]{1,0:T(8,128)(2,1)S(1)}, bf16[16,2048]{1,0:T(8,128)(2,1)S(1)}, u32[]{:S(2)}, u32[]{:S(2)}) collective-permute-start(bf16[16,2048]{1,0:T(8,128)(2,1)S(1)} %constant_dynamic-update-slice_fusion), channel_id=1, source_target_pairs={{0,24},{1,25},{2,26},{3,27},{4,28},{5,29},{6,30},{7,31},{8,16},{9,... | collective-permute-start | bytes 196616 | tf_op jit(solution)/shard_map/ppermute | solution.py:38
  7.8 0.9 %pad_maximum_fusion.1.refs_4_.refs_8_ = bf16[2,512,128]{2,1,0:T(8,128)(2,1)S(1)} fusion(bf16[1,512,128]{2,1,0:T(8,128)(2,1)S(1)} %bitcast.6, bf16[1,512,128]{2,1,0:T(8,128)(2,1)} %bitcast.7), kind=kLoop, calls=%fused_computation.2 | loop fusion | flops 131072 | bytes 524288 | tf_op jit(solution)/shard_map/stack | solution.py:227
  8.8 2.7 %collective-permute-start.6 = (bf16[2,512,128]{2,1,0:T(8,128)(2,1)S(1)}, bf16[2,512,128]{2,1,0:T(8,128)(2,1)S(1)}, u32[]{:S(2)}, u32[]{:S(2)}) collective-permute-start(bf16[2,512,128]{2,1,0:T(8,128)(2,1)S(1)} %pad_maximum_fusion.1.refs_4_.refs_8_), channel_id=1, source_target_pairs={{0,5},{1,4},{2,7},{3,6},{4,1},{5,0},{6,3},{7,2},{8,13},{9,12},{10,... | collective-permute-start | bytes 786440 | tf_op jit(solution)/shard_map/ppermute | solution.py:38
  13.0 6.0 %collective-permute-done.6.refs_7_.refs_11_ = bf16[2,512,128]{2,1,0:T(8,128)(2,1)S(1)} collective-permute-done((bf16[2,512,128]{2,1,0:T(8,128)(2,1)S(1)}, bf16[2,512,128]{2,1,0:T(8,128)(2,1)S(1)}, u32[]{:S(2)}, u32[]{:S(2)}) %collective-permute-start.6) | collective-permute-done | bytes 262176 | tf_op jit(solution)/shard_map/ppermute | solution.py:38
  19.0 4.0 %collective-permute-done.5.refs_6_.refs_10_ = bf16[2,512,128]{2,1,0:T(8,128)(2,1)S(1)} collective-permute-done((bf16[2,512,128]{2,1,0:T(8,128)(2,1)S(1)}, bf16[2,512,128]{2,1,0:T(8,128)(2,1)S(1)}, u32[]{:S(2)}, u32[]{:S(2)}) %collective-permute-start.5) | collective-permute-done | bytes 262176 | tf_op jit(solution)/shard_map/ppermute | solution.py:38
  23.0 4.5 %forward.1 = (f32[3,8,128]{2,1,0:T(8,128)S(1)}, f32[3,8,128]{2,1,0:T(8,128)S(1)}, bf16[1024,128]{1,0:T(8,128)(2,1)S(1)}, bf16[1024,128]{1,0:T(8,128)(2,1)S(1)}) custom-call(s32[1,4]{1,0:T(1,128)S(1)} %copy-done.2, s32[4]{0:T(128)S(1)} %copy-done.3, bf16[64,2048]{1,0:T(8,128)(2,1)S(1)} %pad_maximum_fusion.refs_2_, ...), custom_call_target="tpu_custom_call" | custom-call | tf_op jit(solution)/shard_map/forward/pallas_call | solution.py:237
  27.5 1.2 %collective-permute-done.7 = f32[3,8,128]{2,1,0:T(8,128)S(1)} collective-permute-done((f32[3,8,128]{2,1,0:T(8,128)S(1)}, f32[3,8,128]{2,1,0:T(8,128)S(1)}, u32[]{:S(2)}, u32[]{:S(2)}) %collective-permute-start.7) | collective-permute-done | bytes 12320 | tf_op jit(solution)/shard_map/ppermute | solution.py:38
  28.8 3.6 %collective-permute-start.10 = (f32[3,8,128]{2,1,0:T(8,128)S(1)}, f32[3,8,128]{2,1,0:T(8,128)S(1)}, u32[]{:S(2)}, u32[]{:S(2)}) collective-permute-start(f32[3,8,128]{2,1,0:T(8,128)S(1)} %pad_maximum_fusion.2.refs_4_), channel_id=1, source_target_pairs={{0,24},{1,25},{2,26},{3,27},{4,28},{5,29},{6,30},{7,31},{8,16},{9,... | collective-permute-start | bytes 36872 | tf_op jit(solution)/shard_map/ppermute | solution.py:38
  32.4 0.8 %collective-permute-start.8 = (f32[3,8,128]{2,1,0:T(8,128)S(1)}, f32[3,8,128]{2,1,0:T(8,128)S(1)}, u32[]{:S(2)}, u32[]{:S(2)}) collective-permute-start(f32[3,8,128]{2,1,0:T(8,128)S(1)} %pad_maximum_fusion.2.refs_4_), channel_id=1, source_target_pairs={{0,8},{1,9},{2,10},{3,11},{4,12},{5,13},{6,14},{7,15},{8,0},{9,1},... | collective-permute-start | bytes 36872 | tf_op jit(solution)/shard_map/ppermute | solution.py:38
  33.2 1.1 %collective-permute-done.10.refs_7_ = f32[3,8,128]{2,1,0:T(8,128)S(1)} collective-permute-done((f32[3,8,128]{2,1,0:T(8,128)S(1)}, f32[3,8,128]{2,1,0:T(8,128)S(1)}, u32[]{:S(2)}, u32[]{:S(2)}) %collective-permute-start.10) | collective-permute-done | bytes 12320 | tf_op jit(solution)/shard_map/ppermute | solution.py:38
  34.3 2.6 %collective-permute-done.9.refs_6_ = f32[3,8,128]{2,1,0:T(8,128)S(1)} collective-permute-done((f32[3,8,128]{2,1,0:T(8,128)S(1)}, f32[3,8,128]{2,1,0:T(8,128)S(1)}, u32[]{:S(2)}, u32[]{:S(2)}) %collective-permute-start.9) | collective-permute-done | bytes 12320 | tf_op jit(solution)/shard_map/ppermute | solution.py:38
  37.0 6.1 %backward.1 = (f32[2,512,128]{2,1,0:T(8,128)S(1)}, bf16[2,512,128]{2,1,0:T(8,128)(2,1)S(1)}, bf16[2,512,128]{2,1,0:T(8,128)(2,1)S(1)}, bf16[2,512,128]{2,1,0:T(8...) custom-call(s32[1,4]{1,0:T(1,128)S(1)} %copy-done.2, s32[4]{0:T(128)S(1)} %copy-done.3, ...), custom_call_target="tpu_custom_call" | custom-call | tf_op jit(solution)/shard_map/backward/pallas_call | solution.py:253
  43.1 1.3 %collective-permute-done.11 = bf16[64,1024]{1,0:T(8,128)(2,1)S(1)} collective-permute-done((bf16[64,1024]{1,0:T(8,128)(2,1)S(1)}, bf16[64,1024]{1,0:T(8,128)(2,1)S(1)}, u32[]{:S(2)}, u32[]{:S(2)}) %collective-permute-start.11) | collective-permute-done | bytes 131104 | tf_op jit(solution)/shard_map/ppermute | solution.py:38
  44.6 1.5 %collective-permute-start.15 = (bf16[2,512,128]{2,1,0:T(8,128)(2,1)S(1)}, bf16[2,512,128]{2,1,0:T(8,128)(2,1)S(1)}, u32[]{:S(2)}, u32[]{:S(2)}) collective-permute-start(bf16[2,512,128]{2,1,0:T(8,128)(2,1)S(1)} %get-tuple-element.20), channel_id=1, source_target_pairs={{0,1},{1,0},{2,3},{3,2},{4,5},{5,4},{6,7},{7,6},{8,9},{9,8},{10,11... | collective-permute-start | bytes 786440 | tf_op jit(solution)/shard_map/ppermute | solution.py:38
  46.0 1.5 %collective-permute-start.16 = (bf16[2,512,128]{2,1,0:T(8,128)(2,1)S(1)}, bf16[2,512,128]{2,1,0:T(8,128)(2,1)S(1)}, u32[]{:S(2)}, u32[]{:S(2)}) collective-permute-start(bf16[2,512,128]{2,1,0:T(8,128)(2,1)S(1)} %get-tuple-element.21), channel_id=1, source_target_pairs={{0,4},{1,5},{2,6},{3,7},{4,0},{5,1},{6,2},{7,3},{8,12},{9,13},{10,... | collective-permute-start | bytes 786440 | tf_op jit(solution)/shard_map/ppermute | solution.py:38
  47.5 0.6 collective-permute-start.17
  48.1 3.4 %collective-permute-start.14 = (bf16[16,1024]{1,0:T(8,128)(2,1)S(1)}, bf16[16,1024]{1,0:T(8,128)(2,1)S(1)}, u32[]{:S(2)}, u32[]{:S(2)}) collective-permute-start(bf16[16,1024]{1,0:T(8,128)(2,1)S(1)} %get-tuple-element.30), channel_id=1, source_target_pairs={{0,24},{1,25},{2,26},{3,27},{4,28},{5,29},{6,30},{7,31},{8,16},{9,... | collective-permute-start | bytes 98312 | tf_op jit(solution)/shard_map/ppermute | solution.py:38
  51.5 2.3 %collective-permute-done.14 = bf16[16,1024]{1,0:T(8,128)(2,1)S(1)} collective-permute-done((bf16[16,1024]{1,0:T(8,128)(2,1)S(1)}, bf16[16,1024]{1,0:T(8,128)(2,1)S(1)}, u32[]{:S(2)}, u32[]{:S(2)}) %collective-permute-start.14) | collective-permute-done | bytes 32800 | tf_op jit(solution)/shard_map/ppermute | solution.py:38
  53.8 2.5 %collective-permute-done.13 = bf16[16,1024]{1,0:T(8,128)(2,1)S(1)} collective-permute-done((bf16[16,1024]{1,0:T(8,128)(2,1)S(1)}, bf16[16,1024]{1,0:T(8,128)(2,1)S(1)}, u32[]{:S(2)}, u32[]{:S(2)}) %collective-permute-start.13) | collective-permute-done | bytes 32800 | tf_op jit(solution)/shard_map/ppermute | solution.py:38
  56.4 0.6 %fusion.2 = bf16[16,1024]{1,0:T(8,128)(2,1)} fusion(f32[64,1024]{1,0:T(8,128)S(1)} %get-tuple-element.24, bf16[16,1024]{1,0:T(8,128)(2,1)S(1)} %collective-permute-done.14, bf16[16,1024]{1,0:T(8,128)(2,1)S(1)} %collective-permute-done.13, bf16[16,1024]{1,0:T(8,128)(2,1)S(1)} %collective-permute-done.12), kind=kLoop, calls=%fused_computation.9 | loop fusion | flops 114688 | bytes 196608 | tf_op jit(solution)/shard_map/convert_element_type | solution.py:283
  57.0 2.8 %collective-permute-done.17 = bf16[2,512,128]{2,1,0:T(8,128)(2,1)S(1)} collective-permute-done((bf16[2,512,128]{2,1,0:T(8,128)(2,1)S(1)}, bf16[2,512,128]{2,1,0:T(8,128)(2,1)S(1)}, u32[]{:S(2)}, u32[]{:S(2)}) %collective-permute-start.17) | collective-permute-done | bytes 262176 | tf_op jit(solution)/shard_map/ppermute | solution.py:38
  59.9 0.7 %slice_bitcast_fusion = (bf16[512,128]{1,0:T(8,128)(2,1)}, bf16[512,128]{1,0:T(8,128)(2,1)}) fusion(bf16[2,512,128]{2,1,0:T(8,128)(2,1)S(1)} %add_convert_fusion), kind=kLoop, calls=%fused_computation.4 | loop fusion | bytes 524288 | tf_op jit(solution)/shard_map/convert_element_type | solution.py:285
  (36 shorter events, 2.4 us)
Async XLA Ops:
  0.6 7.2 %copy-start.4 = (bf16[512,128]{1,0:T(8,128)(2,1)S(1)}, bf16[512,128]{1,0:T(8,128)(2,1)}, u32[]{:S(2)}) copy-start(bf16[512,128]{1,0:T(8,128)(2,1)} %param.11) | copy-start | bytes 393220
  2.2 9.9 %collective-permute-start.2 = (bf16[16,2048]{1,0:T(8,128)(2,1)S(1)}, bf16[16,2048]{1,0:T(8,128)(2,1)S(1)}, u32[]{:S(2)}, u32[]{:S(2)}) collective-permute-start(bf16[16,2048]{1,0:T(8,128)(2,1)S(1)} %constant_dynamic-update-slice_fusion), channel_id=1, source_target_pairs={{0,24},{1,25},{2,26},{3,27},{4,28},{5,29},{6,30},{7,31},{8,16},{9,... | collective-permute-start | bytes 196616 | tf_op jit(solution)/shard_map/ppermute | solution.py:38
  7.3 5.6 %collective-permute-start.1 = (bf16[16,2048]{1,0:T(8,128)(2,1)S(1)}, bf16[16,2048]{1,0:T(8,128)(2,1)S(1)}, u32[]{:S(2)}, u32[]{:S(2)}) collective-permute-start(bf16[16,2048]{1,0:T(8,128)(2,1)S(1)} %constant_dynamic-update-slice_fusion), channel_id=1, source_target_pairs={{0,16},{1,17},{2,18},{3,19},{4,20},{5,21},{6,22},{7,23},{8,24},{9,... | collective-permute-start | bytes 196616 | tf_op jit(solution)/shard_map/ppermute | solution.py:38
  7.3 5.6 %collective-permute-start = (bf16[16,2048]{1,0:T(8,128)(2,1)S(1)}, bf16[16,2048]{1,0:T(8,128)(2,1)S(1)}, u32[]{:S(2)}, u32[]{:S(2)}) collective-permute-start(bf16[16,2048]{1,0:T(8,128)(2,1)S(1)} %constant_dynamic-update-slice_fusion), channel_id=1, source_target_pairs={{0,8},{1,9},{2,10},{3,11},{4,12},{5,13},{6,14},{7,15},{8,0},{9,1},... | collective-permute-start | bytes 196616 | tf_op jit(solution)/shard_map/ppermute | solution.py:38
  8.8 14.2 %copy-start = (bf16[256,128]{1,0:T(8,128)(2,1)S(1)}, bf16[256,128]{1,0:T(8,128)(2,1)}, u32[]{:S(2)}) copy-start(bf16[256,128]{1,0:T(8,128)(2,1)} %refs_12_.1) | copy-start | bytes 196612
  8.8 14.2 %copy-start.1 = (bf16[256,128]{1,0:T(8,128)(2,1)S(1)}, bf16[256,128]{1,0:T(8,128)(2,1)}, u32[]{:S(2)}) copy-start(bf16[256,128]{1,0:T(8,128)(2,1)} %refs_13_.1) | copy-start | bytes 196612
  8.8 14.2 %copy-start.2 = (s32[1,4]{1,0:T(1,128)S(1)}, s32[1,4]{1,0:T(1,128)}, u32[]{:S(2)}) copy-start(s32[1,4]{1,0:T(1,128)} %refs_0_.3) | copy-start | bytes 52
  8.8 14.2 %copy-start.3 = (s32[4]{0:T(128)S(1)}, s32[4]{0:T(128)}, u32[]{:S(2)}) copy-start(s32[4]{0:T(128)} %refs_1_.3) | copy-start | bytes 52
  8.8 10.2 %collective-permute-start.6 = (bf16[2,512,128]{2,1,0:T(8,128)(2,1)S(1)}, bf16[2,512,128]{2,1,0:T(8,128)(2,1)S(1)}, u32[]{:S(2)}, u32[]{:S(2)}) collective-permute-start(bf16[2,512,128]{2,1,0:T(8,128)(2,1)S(1)} %pad_maximum_fusion.1.refs_4_.refs_8_), channel_id=1, source_target_pairs={{0,5},{1,4},{2,7},{3,6},{4,1},{5,0},{6,3},{7,2},{8,13},{9,12},{10,... | collective-permute-start | bytes 786440 | tf_op jit(solution)/shard_map/ppermute | solution.py:38
  11.6 11.4 %collective-permute-start.5 = (bf16[2,512,128]{2,1,0:T(8,128)(2,1)S(1)}, bf16[2,512,128]{2,1,0:T(8,128)(2,1)S(1)}, u32[]{:S(2)}, u32[]{:S(2)}) collective-permute-start(bf16[2,512,128]{2,1,0:T(8,128)(2,1)S(1)} %pad_maximum_fusion.1.refs_4_.refs_8_), channel_id=1, source_target_pairs={{0,4},{1,5},{2,6},{3,7},{4,0},{5,1},{6,2},{7,3},{8,12},{9,13},{10,... | collective-permute-start | bytes 786440 | tf_op jit(solution)/shard_map/ppermute | solution.py:38
  12.1 10.9 %collective-permute-start.4 = (bf16[2,512,128]{2,1,0:T(8,128)(2,1)S(1)}, bf16[2,512,128]{2,1,0:T(8,128)(2,1)S(1)}, u32[]{:S(2)}, u32[]{:S(2)}) collective-permute-start(bf16[2,512,128]{2,1,0:T(8,128)(2,1)S(1)} %pad_maximum_fusion.1.refs_4_.refs_8_), channel_id=1, source_target_pairs={{0,1},{1,0},{2,3},{3,2},{4,5},{5,4},{6,7},{7,6},{8,9},{9,8},{10,11... | collective-permute-start | bytes 786440 | tf_op jit(solution)/shard_map/ppermute | solution.py:38
  12.9 10.1 %collective-permute-start.3 = (bf16[64,2048]{1,0:T(8,128)(2,1)S(1)}, bf16[64,2048]{1,0:T(8,128)(2,1)S(1)}, u32[]{:S(2)}, u32[]{:S(2)}) collective-permute-start(bf16[64,2048]{1,0:T(8,128)(2,1)S(1)} %pad_maximum_fusion.refs_2_), channel_id=1, source_target_pairs={{0,2},{1,3},{2,0},{3,1},{4,6},{5,7},{6,4},{7,5},{8,10},{9,11},{10,... | collective-permute-start | bytes 786440 | tf_op jit(solution)/shard_map/ppermute | solution.py:38
  27.5 1.2 %collective-permute-start.7 = (f32[3,8,128]{2,1,0:T(8,128)S(1)}, f32[3,8,128]{2,1,0:T(8,128)S(1)}, u32[]{:S(2)}, u32[]{:S(2)}) collective-permute-start(f32[3,8,128]{2,1,0:T(8,128)S(1)} %get-tuple-element.16), channel_id=1, source_target_pairs={{0,2},{1,3},{2,0},{3,1},{4,6},{5,7},{6,4},{7,5},{8,10},{9,11},{10,... | collective-permute-start | bytes 36872 | tf_op jit(solution)/shard_map/ppermute | solution.py:38
  28.8 5.6 %collective-permute-start.10 = (f32[3,8,128]{2,1,0:T(8,128)S(1)}, f32[3,8,128]{2,1,0:T(8,128)S(1)}, u32[]{:S(2)}, u32[]{:S(2)}) collective-permute-start(f32[3,8,128]{2,1,0:T(8,128)S(1)} %pad_maximum_fusion.2.refs_4_), channel_id=1, source_target_pairs={{0,24},{1,25},{2,26},{3,27},{4,28},{5,29},{6,30},{7,31},{8,16},{9,... | collective-permute-start | bytes 36872 | tf_op jit(solution)/shard_map/ppermute | solution.py:38
  32.4 4.6 %collective-permute-start.9 = (f32[3,8,128]{2,1,0:T(8,128)S(1)}, f32[3,8,128]{2,1,0:T(8,128)S(1)}, u32[]{:S(2)}, u32[]{:S(2)}) collective-permute-start(f32[3,8,128]{2,1,0:T(8,128)S(1)} %pad_maximum_fusion.2.refs_4_), channel_id=1, source_target_pairs={{0,16},{1,17},{2,18},{3,19},{4,20},{5,21},{6,22},{7,23},{8,24},{9,... | collective-permute-start | bytes 36872 | tf_op jit(solution)/shard_map/ppermute | solution.py:38
  32.4 4.6 %collective-permute-start.8 = (f32[3,8,128]{2,1,0:T(8,128)S(1)}, f32[3,8,128]{2,1,0:T(8,128)S(1)}, u32[]{:S(2)}, u32[]{:S(2)}) collective-permute-start(f32[3,8,128]{2,1,0:T(8,128)S(1)} %pad_maximum_fusion.2.refs_4_), channel_id=1, source_target_pairs={{0,8},{1,9},{2,10},{3,11},{4,12},{5,13},{6,14},{7,15},{8,0},{9,1},... | collective-permute-start | bytes 36872 | tf_op jit(solution)/shard_map/ppermute | solution.py:38
  43.0 1.4 %collective-permute-start.11 = (bf16[64,1024]{1,0:T(8,128)(2,1)S(1)}, bf16[64,1024]{1,0:T(8,128)(2,1)S(1)}, u32[]{:S(2)}, u32[]{:S(2)}) collective-permute-start(bf16[64,1024]{1,0:T(8,128)(2,1)S(1)} %get-tuple-element.18), channel_id=1, source_target_pairs={{0,2},{1,3},{2,0},{3,1},{4,6},{5,7},{6,4},{7,5},{8,10},{9,11},{10,... | collective-permute-start | bytes 393224 | tf_op jit(solution)/shard_map/ppermute | solution.py:38
  44.5 7.0 %collective-permute-start.12 = (bf16[16,1024]{1,0:T(8,128)(2,1)S(1)}, bf16[16,1024]{1,0:T(8,128)(2,1)S(1)}, u32[]{:S(2)}, u32[]{:S(2)}) collective-permute-start(bf16[16,1024]{1,0:T(8,128)(2,1)S(1)} %get-tuple-element.29), channel_id=1, source_target_pairs={{0,8},{1,9},{2,10},{3,11},{4,12},{5,13},{6,14},{7,15},{8,0},{9,1},... | collective-permute-start | bytes 98312 | tf_op jit(solution)/shard_map/ppermute | solution.py:38
  44.6 12.4 %collective-permute-start.15 = (bf16[2,512,128]{2,1,0:T(8,128)(2,1)S(1)}, bf16[2,512,128]{2,1,0:T(8,128)(2,1)S(1)}, u32[]{:S(2)}, u32[]{:S(2)}) collective-permute-start(bf16[2,512,128]{2,1,0:T(8,128)(2,1)S(1)} %get-tuple-element.20), channel_id=1, source_target_pairs={{0,1},{1,0},{2,3},{3,2},{4,5},{5,4},{6,7},{7,6},{8,9},{9,8},{10,11... | collective-permute-start | bytes 786440 | tf_op jit(solution)/shard_map/ppermute | solution.py:38
  46.0 10.9 %collective-permute-start.16 = (bf16[2,512,128]{2,1,0:T(8,128)(2,1)S(1)}, bf16[2,512,128]{2,1,0:T(8,128)(2,1)S(1)}, u32[]{:S(2)}, u32[]{:S(2)}) collective-permute-start(bf16[2,512,128]{2,1,0:T(8,128)(2,1)S(1)} %get-tuple-element.21), channel_id=1, source_target_pairs={{0,4},{1,5},{2,6},{3,7},{4,0},{5,1},{6,2},{7,3},{8,12},{9,13},{10,... | collective-permute-start | bytes 786440 | tf_op jit(solution)/shard_map/ppermute | solution.py:38
  47.5 12.3 %collective-permute-start.17 = (bf16[2,512,128]{2,1,0:T(8,128)(2,1)S(1)}, bf16[2,512,128]{2,1,0:T(8,128)(2,1)S(1)}, u32[]{:S(2)}, u32[]{:S(2)}) collective-permute-start(bf16[2,512,128]{2,1,0:T(8,128)(2,1)S(1)} %get-tuple-element.22), channel_id=1, source_target_pairs={{0,5},{1,4},{2,7},{3,6},{4,1},{5,0},{6,3},{7,2},{8,13},{9,12},{10,... | collective-permute-start | bytes 786440 | tf_op jit(solution)/shard_map/ppermute | solution.py:38
  48.1 5.7 %collective-permute-start.14 = (bf16[16,1024]{1,0:T(8,128)(2,1)S(1)}, bf16[16,1024]{1,0:T(8,128)(2,1)S(1)}, u32[]{:S(2)}, u32[]{:S(2)}) collective-permute-start(bf16[16,1024]{1,0:T(8,128)(2,1)S(1)} %get-tuple-element.30), channel_id=1, source_target_pairs={{0,24},{1,25},{2,26},{3,27},{4,28},{5,29},{6,30},{7,31},{8,16},{9,... | collective-permute-start | bytes 98312 | tf_op jit(solution)/shard_map/ppermute | solution.py:38
  51.5 4.8 %collective-permute-start.13 = (bf16[16,1024]{1,0:T(8,128)(2,1)S(1)}, bf16[16,1024]{1,0:T(8,128)(2,1)S(1)}, u32[]{:S(2)}, u32[]{:S(2)}) collective-permute-start(bf16[16,1024]{1,0:T(8,128)(2,1)S(1)} %get-tuple-element.31), channel_id=1, source_target_pairs={{0,16},{1,17},{2,18},{3,19},{4,20},{5,21},{6,22},{7,23},{8,24},{9,... | collective-permute-start | bytes 98312 | tf_op jit(solution)/shard_map/ppermute | solution.py:38
